TPU v7x, 128 devices: a whole 4x4x4 slice. The times are simulated.
128 devices in a mesh: stream: 4 (over x), cross: 32 (over y, z, core).
Axes of the slice: x: 4, y: 4, z: 4, core: 2. Of those that a mesh axis runs over, the one named last changes fastest.
Arguments:
- velocity: bfloat16 [128, 3, 48, 256, 128], P(None, None, 'stream', 'cross'), may hold values from -40 to 40, as said below
- metric_x: float32 [48], P('stream'), may hold values from 0.5 to 2
- metric_y: float32 [256], P('cross'), may hold values from 0.5 to 2
- metric_z: float32 [128], replicated, may hold values from 0.5 to 2
Outputs:
- modes: bfloat16 [128, 4, 48, 256, 128], P(None, None, 'stream', 'cross')
- factor: float32 [128, 128], replicated
Inputs may be any that keep to these rules, and one draw needn't show every extreme that they name: velocity snapshots share a common part across snapshots.
All inputs are finite; a program needn't handle non-finite values.
Results may differ from a plain program's by a relative error of at most 0.0023.
The roundings to bfloat16 on the way count: a program that leaves them out, or rounds other values in their place, can miss the bound.
Values may be sent and summed in bfloat16 or wider, within the bound.
A program may use at most 128 MiB of HBM per device.

v0:
```python
import jax
import jax.numpy as jnp
from jax import lax
from jax.sharding import PartitionSpec as P


def with_halo(cells, sides, width):
    for axis, dim in sides:
        count = lax.axis_size(axis)
        ends = count - 1
        head = lax.slice_in_dim(cells, 0, width, axis=dim)
        tail = lax.slice_in_dim(cells, cells.shape[dim] - width, cells.shape[dim], axis=dim)
        cells = jnp.concatenate(
            [
                lax.ppermute(tail, axis, [(i, (i + 1) % count) for i in range(ends)]),
                cells,
                lax.ppermute(head, axis, [((i + 1) % count, i) for i in range(ends)]),
            ],
            axis=dim,
        )
    return cells


def central(padded, axis):
    count = padded.shape[axis] - 4

    def part_at(offset):
        return lax.slice_in_dim(padded, offset, offset + count, axis=axis)

    return (8.0 * (part_at(3) - part_at(1)) - (part_at(4) - part_at(0))) / 12.0


def fields(along_x, along_y, interior, metric_x, metric_y, metric_z):

    def deriv_x(comp):
        return central(along_x[:, comp].astype(jnp.float32), 1) * metric_x[:, None, None]

    def deriv_y(comp):
        return central(along_y[:, comp].astype(jnp.float32), 2) * metric_y[:, None]

    def deriv_z(comp):
        inner = interior[:, comp].astype(jnp.float32)
        return central(jnp.pad(inner, ((0, 0), (0, 0), (0, 0), (2, 2))), 3) * metric_z

    vort_x = deriv_y(2) - deriv_z(1)
    vort_y = deriv_z(0) - deriv_x(2)
    vort_z = deriv_x(1) - deriv_y(0)
    dilatation = deriv_x(0) + deriv_y(1) + deriv_z(2)
    return jnp.stack([vort_x, vort_y, vort_z, dilatation], axis=1).astype(jnp.bfloat16)


def inner_products(flat):
    return lax.dot_general(flat, flat, (((1,), (1,)), ((), ())), preferred_element_type=jnp.float32)


def global_factor(flat, scale):
    local = inner_products(flat)
    gram = lax.psum(local, ("stream", "cross"))
    lower = jnp.linalg.cholesky(gram * scale)
    return lower


def shards(velocity, metric_x, metric_y, metric_z):
    snaps, comps, cells_x, cells_y, cells_z = velocity.shape
    groups = snaps // 8
    padded = with_halo(velocity, (("stream", 2), ("cross", 3)), 2)
    padded_groups = padded.reshape(groups, 8, comps, cells_x + 4, cells_y + 4, cells_z)

    def one_block(block):
        return fields(
            block[:, :, :, 2:-2, :],
            block[:, :, 2:-2, :, :],
            block[:, :, 2:-2, 2:-2, :],
            metric_x,
            metric_y,
            metric_z,
        )

    stacked = lax.map(one_block, padded_groups)
    flat = stacked.reshape(snaps, 4 * cells_x * cells_y * cells_z)
    total_rows = (
        4.0 * cells_x * lax.axis_size("stream") * cells_y * lax.axis_size("cross") * cells_z
    )
    scale = 1.0 / total_rows
    lower = global_factor(flat, scale)
    identity = jnp.eye(snaps, dtype=jnp.float32)
    inverse = jax.scipy.linalg.solve_triangular(lower, identity, lower=True)
    basis = jnp.dot(inverse.astype(jnp.bfloat16), flat, preferred_element_type=jnp.float32).astype(
        jnp.bfloat16
    )
    return (basis.reshape(snaps, 4, cells_x, cells_y, cells_z), lower)


def solution(mesh):
    return jax.shard_map(
        shards,
        mesh=mesh,
        in_specs=(P(None, None, "stream", "cross", None), P("stream"), P("cross"), P()),
        out_specs=(P(None, None, "stream", "cross", None), P()),
        check_vma=False,
    )
```

profile of v0, /device:TPU:1, one launch (start us, length us, event | category | flops | bytes accessed | tf_op | source)
XLA Modules:
  0.0 442.5 jit_solution(3186469633887773172)
XLA Ops:
  7.2 7.0 %copy.14 = bf16[128,3,12,8,128]{4,2,3,1,0:T(8,128)(2,1)S(1)} copy(bf16[128,3,12,8,128]{4,3,2,1,0:T(8,128)(2,1)} %param.6) | data formatting | bytes 18874368 | tf_op args[0]
  14.2 3.0 fusion.49
  17.2 4.0 collective-permute-start
  21.3 1.3 collective-permute-start.1
  22.6 31.7 %collective-permute-done = bf16[128,3,2,8,128]{4,2,3,1,0:T(2,128)(2,1)S(1)} collective-permute-done((bf16[128,3,2,8,128]{4,2,3,1,0:T(2,128)(2,1)S(1)}, bf16[128,3,2,8,128]{4,2,3,1,0:T(2,128)(2,1)S(1)}, u32[]{:S(2)}, u32[]{:S(2)}) %collective-permute-start) | collective-permute-done | bytes 1572896 | tf_op jit(solution)/shard_map/ppermute | solution.py:15
  54.3 3.9 collective-permute-done.1
  58.2 6.2 %pad_maximum_fusion.3 = (bf16[128,3,16,2,128]{4,2,3,1,0:T(8,128)(2,1)}, bf16[128,3,16,2,128]{4,2,3,1,0:T(8,128)(2,1)}) fusion(bf16[128,3,2,8,128]{4,2,3,1,0:T(2,128)(2,1)S(1)} %collective-permute-done.1, bf16[128,3,12,8,128]{4,2,3,1,0:T(8,128)(2,1)S(1)} %copy.14, bf16[128,3,2,8,128]{4,2,3,1,0:T(2,128)(2,1)S(1)} %collective-permute-done), kind=kLoop, calls=%fused_computation.87 | loop fusion | flops 18874368 | bytes 18874368 | tf_op jit(solution)/shard_map/slice | solution.py:12
  64.4 5.2 %collective-permute-start.2 = (bf16[128,3,16,2,128]{4,2,3,1,0:T(8,128)(2,1)}, bf16[128,3,16,2,128]{4,2,3,1,0:T(8,128)(2,1)}, u32[]{:S(2)}, u32[]{:S(2)}) collective-permute-start(bf16[128,3,16,2,128]{4,2,3,1,0:T(8,128)(2,1)} %get-tuple-element.113), channel_id=1, source_target_pairs={{0,1},{1,2},{2,3},{3,4},{4,5},{5,6},{6,7},{7,8},{8,9},{9,10},{10,1... | collective-permute-start | bytes 9437192 | tf_op jit(solution)/shard_map/ppermute | solution.py:15
  69.6 1.9 collective-permute-start.3
  71.6 32.5 %collective-permute-done.2 = bf16[128,3,16,2,128]{4,2,3,1,0:T(8,128)(2,1)} collective-permute-done((bf16[128,3,16,2,128]{4,2,3,1,0:T(8,128)(2,1)}, bf16[128,3,16,2,128]{4,2,3,1,0:T(8,128)(2,1)}, u32[]{:S(2)}, u32[]{:S(2)}) %collective-permute-start.2) | collective-permute-done | bytes 3145760 | tf_op jit(solution)/shard_map/ppermute | solution.py:15
  104.2 4.4 collective-permute-done.3
  108.6 19.7 %pad_maximum_fusion = bf16[128,3,16,12,128]{4,2,3,1,0:T(8,128)(2,1)} fusion(bf16[128,3,16,2,128]{4,2,3,1,0:T(8,128)(2,1)} %collective-permute-done.3, bf16[128,3,2,8,128]{4,2,3,1,0:T(2,128)(2,1)S(1)} %collective-permute-done.1, bf16[128,3,12,8,128]{4,2,3,1,0:T(8,128)(2,1)} %copy-done, bf16[128,3,2,8,128]{4,2,3,1,0:T(2,128)(2,1)S(1)} %collective-permute-done, ...), kind=kLoop, calls=%fused_computation.83 | loop fusion | flops 94371840 | bytes 37748736 | tf_op jit(solution)/shard_map/concatenate | solution.py:13
  128.2 87.1 %while.12 = (s32[]{:T(128)}, bf16[16,8,4,12,8,128]{5,4,3,2,1,0:T(8,128)(2,1)}, bf16[16,8,3,16,12,128]{5,3,4,2,1,0:T(8,128)(2,1)}, f32[8]{0:T(128)S(1)}, f32[128]{0:T(128)S(1)}, /*index=5*/f32[12]{0:T(128)S(1)}, s32[]{:T(128)}) while((s32[]{:T(128)}, bf16[16,8,4,12,8,128]{5,4,3,2,1,0:T(8,128)(2,1)}, ...), condition=%wide.region_1.2_spmd, body=%wide.region_0.1_spmd.sunk | while | flops 9594006 | bytes 29236672 | solution.py:79
  128.2 1.5 constant_dynamic-slice_fusion.2
  131.1 0.5 fusion.63
  132.7 0.9 maximum_dynamic-update-slice_fusion.2
  133.7 1.5 constant_dynamic-slice_fusion.2
  136.5 0.5 fusion.63
  138.2 0.9 maximum_dynamic-update-slice_fusion.2
  139.1 1.5 constant_dynamic-slice_fusion.2
  141.9 0.5 fusion.63
  143.6 0.9 maximum_dynamic-update-slice_fusion.2
  144.6 1.5 constant_dynamic-slice_fusion.2
  147.4 0.5 fusion.63
  149.1 0.9 maximum_dynamic-update-slice_fusion.2
  150.0 1.5 constant_dynamic-slice_fusion.2
  152.8 0.5 fusion.63
  154.5 0.9 maximum_dynamic-update-slice_fusion.2
  155.4 1.5 constant_dynamic-slice_fusion.2
  158.3 0.5 fusion.63
  159.9 0.9 maximum_dynamic-update-slice_fusion.2
  160.9 1.5 constant_dynamic-slice_fusion.2
  163.7 0.5 fusion.63
  165.4 0.9 maximum_dynamic-update-slice_fusion.2
  166.3 1.5 constant_dynamic-slice_fusion.2
  169.1 0.5 fusion.63
  170.8 0.9 maximum_dynamic-update-slice_fusion.2
  171.8 1.5 constant_dynamic-slice_fusion.2
  176.3 0.9 maximum_dynamic-update-slice_fusion.2
  177.2 1.5 constant_dynamic-slice_fusion.2
  181.7 0.9 maximum_dynamic-update-slice_fusion.2
  182.6 1.5 constant_dynamic-slice_fusion.2
  187.1 0.9 maximum_dynamic-update-slice_fusion.2
  188.1 1.5 constant_dynamic-slice_fusion.2
  192.6 0.9 maximum_dynamic-update-slice_fusion.2
  193.5 1.5 constant_dynamic-slice_fusion.2
  198.0 0.9 maximum_dynamic-update-slice_fusion.2
  199.0 1.5 constant_dynamic-slice_fusion.2
  203.5 0.9 maximum_dynamic-update-slice_fusion.2
  204.4 1.5 constant_dynamic-slice_fusion.2
  208.9 0.9 maximum_dynamic-update-slice_fusion.2
  209.8 1.5 constant_dynamic-slice_fusion.2
  214.3 0.9 maximum_dynamic-update-slice_fusion.2
  215.3 17.0 %reshape.120 = bf16[128,49152]{1,0:T(8,128)(2,1)} reshape(bf16[16,8,4,12,8,128]{5,4,3,2,1,0:T(8,128)(2,1)} %get-tuple-element.79) | data formatting | bytes 25165824 | tf_op jit(solution)/shard_map/reshape | solution.py:80
  232.3 12.2 %fusion.50 = f32[128,128]{0,1:T(8,128)} fusion(bf16[128,49152]{1,0:T(8,128)(2,1)} %reshape.120), kind=kOutput, calls=%fused_computation.100 | convolution fusion | flops 1610612736 | bytes 12648448 | tf_op jit(solution)/shard_map/dot_general | solution.py:53
  244.5 141.5 %all-reduce.5.cloned.1.call-done = f32[128,128]{0,1:T(8,128)} async-done(((f32[128,128]{0,1:T(8,128)}), f32[128,128]{0,1:T(8,128)}) %all-reduce.5.cloned.1.call-update) | async-done | bytes 65552 | tf_op jit(solution)/shard_map/psum | solution.py:58
  386.0 0.8 broadcast_multiply_fusion.3
  387.0 0.9 fusion.48
  387.8 11.7 %cholesky.17 = f32[128,128]{1,0:T(8,128)S(1)} custom-call(f32[128,128]{1,0:T(8,128)S(1)} %fusion.48), custom_call_target="Cholesky" | custom-call | tf_op jit(solution)/shard_map/jit(cholesky)/cholesky | solution.py:59
  399.6 0.6 compare_reduce_fusion
  400.2 1.3 select_bitcast_fusion
  401.5 9.8 %custom-call.7 = f32[1,128,128]{1,2,0:T(8,128)S(1)} custom-call(f32[1,128,128]{2,1,0:T(8,128)S(1)} %get-tuple-element.98), custom_call_target="InvertDiagBlocksLowerTriangular" | custom-call | tf_op jit(solution)/shard_map/jit(_solve_triangular)/triangular_solve | solution.py:87
  411.6 12.5 %fusion.46 = bf16[16,8,384,128]{3,1,2,0:T(8,128)(2,1)} fusion(bf16[128,128]{1,0:T(8,128)(2,1)S(1)} %convolution_convert_fusion.1, bf16[128,49152]{1,0:T(8,128)(2,1)} %reshape.120), kind=kOutput, calls=%fused_computation.84 | convolution fusion | flops 1616904192 | bytes 25198592 | tf_op jit(solution)/shard_map/dot_general | solution.py:88
  424.1 11.6 %copy.22 = bf16[16,8,384,128]{3,2,1,0:T(8,128)(2,1)} copy(bf16[16,8,384,128]{3,1,2,0:T(8,128)(2,1)} %fusion.46) | data formatting | bytes 25165824
  (198 shorter events, 43.3 us)
Async XLA Ops:
  7.2 378.9 %all-reduce.5.cloned.1.call-start = ((), (), s32[]{:S(2)}) async-start(), calls=%async_computation | async-start | bytes 131072 | tf_op jit(solution)/shard_map/psum | solution.py:58
  14.2 50.2 %copy-start = (bf16[128,3,12,8,128]{4,2,3,1,0:T(8,128)(2,1)}, bf16[128,3,12,8,128]{4,2,3,1,0:T(8,128)(2,1)S(1)}, u32[]{:S(2)}) copy-start(bf16[128,3,12,8,128]{4,2,3,1,0:T(8,128)(2,1)S(1)} %copy.14) | copy-start | bytes 28311556
  17.2 37.0 %collective-permute-start = (bf16[128,3,2,8,128]{4,2,3,1,0:T(2,128)(2,1)S(1)}, bf16[128,3,2,8,128]{4,2,3,1,0:T(2,128)(2,1)S(1)}, u32[]{:S(2)}, u32[]{:S(2)}) collective-permute-start(bf16[128,3,2,8,128]{4,2,3,1,0:T(2,128)(2,1)S(1)} %get-tuple-element.115), channel_id=1, source_target_pairs={{0,32},{32,64},{64,96},{1,33},{33,65},{65,97},{2,34},{34,66},{66,9... | collective-permute-start | bytes 4718600 | tf_op jit(solution)/shard_map/ppermute | solution.py:15
  21.3 36.9 %collective-permute-start.1 = (bf16[128,3,2,8,128]{4,2,3,1,0:T(2,128)(2,1)S(1)}, bf16[128,3,2,8,128]{4,2,3,1,0:T(2,128)(2,1)S(1)}, u32[]{:S(2)}, u32[]{:S(2)}) collective-permute-start(bf16[128,3,2,8,128]{4,2,3,1,0:T(2,128)(2,1)S(1)} %get-tuple-element.116), channel_id=1, source_target_pairs={{32,0},{64,32},{96,64},{33,1},{65,33},{97,65},{34,2},{66,34},{98,6... | collective-permute-start | bytes 4718600 | tf_op jit(solution)/shard_map/ppermute | solution.py:17
  64.4 39.7 %collective-permute-start.2 = (bf16[128,3,16,2,128]{4,2,3,1,0:T(8,128)(2,1)}, bf16[128,3,16,2,128]{4,2,3,1,0:T(8,128)(2,1)}, u32[]{:S(2)}, u32[]{:S(2)}) collective-permute-start(bf16[128,3,16,2,128]{4,2,3,1,0:T(8,128)(2,1)} %get-tuple-element.113), channel_id=1, source_target_pairs={{0,1},{1,2},{2,3},{3,4},{4,5},{5,6},{6,7},{7,8},{8,9},{9,10},{10,1... | collective-permute-start | bytes 9437192 | tf_op jit(solution)/shard_map/ppermute | solution.py:15
  69.6 38.9 %collective-permute-start.3 = (bf16[128,3,16,2,128]{4,2,3,1,0:T(8,128)(2,1)}, bf16[128,3,16,2,128]{4,2,3,1,0:T(8,128)(2,1)}, u32[]{:S(2)}, u32[]{:S(2)}) collective-permute-start(bf16[128,3,16,2,128]{4,2,3,1,0:T(8,128)(2,1)} %get-tuple-element.114), channel_id=1, source_target_pairs={{1,0},{2,1},{3,2},{4,3},{5,4},{6,5},{7,6},{8,7},{9,8},{10,9},{11,1... | collective-permute-start | bytes 9437192 | tf_op jit(solution)/shard_map/ppermute | solution.py:17
  71.6 56.6 %copy-start.1 = (f32[8]{0:T(128)S(1)}, f32[8]{0:T(128)}, u32[]{:S(2)}) copy-start(f32[8]{0:T(128)} %param.8) | copy-start | bytes 100
  71.6 56.6 %copy-start.2 = (f32[128]{0:T(128)S(1)}, f32[128]{0:T(128)}, u32[]{:S(2)}) copy-start(f32[128]{0:T(128)} %param.9) | copy-start | bytes 1540
  71.6 56.6 %copy-start.3 = (f32[12]{0:T(128)S(1)}, f32[12]{0:T(128)}, u32[]{:S(2)}) copy-start(f32[12]{0:T(128)} %param.7) | copy-start | bytes 148
Sparse Core Ops, SparseCore 0:
  244.7 141.3 all-reduce.4
where the time goes:
time: 444 us; the launch traced here: 442 us
  waiting for transfers between devices  214 us (48%)
  other arithmetic  104 us (23%)
  local copies, waits for them, and re-layouts  71.8 us (16%)
  matrix products  24.9 us (6%)
  between operations  14.1 us (3%)
  starting transfers between devices  12.5 us (3%)
    psum x1, waiting for transfers between devices, global_factor(): gram = lax.psum(local, ('stream', 'cross'))  141 us
    ppermute x2, waiting for transfers between devices, with_halo(): lax.ppermute(tail, axis, [(i, (i + 1) % count) for i in range(ends)])  64.2 us
    dynamic_slice x32, local copies, waits for them, and re-layouts, shards(): stacked = lax.map(one_block, padded_groups)  30 us
    another operation x48, other arithmetic, fields(): jnp.stack([vort_x, vort_y, vort_z, dilatation], axis=1).astype(jnp.bfloat16)  21.7 us
    concatenate x1, other arithmetic, with_halo(): jnp.concatenate([lax.ppermute(tail, axis, [(i, (i + 1) % count) for i in...  19.7 us
    unnamed x10, local copies, waits for them, and re-layouts  18.6 us
    reshape x1, local copies, waits for them, and re-layouts, shards(): flat = stacked.reshape(snaps, 4 * cells_x * cells_y * cells_z)  17 us
    dynamic_update_slice x16, other arithmetic, shards(): stacked = lax.map(one_block, padded_groups)  15 us
  transfers between devices with their start and end apart: 5, of which 5 were waited for; matrix products, arithmetic and copies ran while one was open for 0% of the time, Pallas kernels for 0%

commit v1 on v0

v1 whole, which is shorter than its diff:
```python
import functools

import jax
import jax.numpy as jnp
from jax import lax
from jax.experimental import pallas as pl
from jax.experimental.pallas import tpu as pltpu
from jax.sharding import PartitionSpec as P

MESH = pl.DeviceIdType.MESH
F32 = jnp.float32
BF16 = jnp.bfloat16
VMEM_LIMIT = 60 * 1024 * 1024
PANEL = 8


def gram_kernel(
    sizes, vel, mx, my, mz, sz, x_out, gram_out,
    raw, tiles, stack, wide, dz, acc, half, part, whole,
    load_sem, out_sem, xs_sem, xr_sem, xs2_sem, xr2_sem, ys_sem, yr_sem,
    cs_sem, cr_sem, as_sem, ar_sem, fs_sem, fr_sem,
):
    nx, ny, nz = sizes
    comps, xp, yp, snaps, cz = tiles.shape
    xl, yl = xp - 4, yp - 4
    nc = ny * nz * 2
    sx = lax.axis_index("stream")
    cr = lax.axis_index("cross")
    core = cr % 2
    iz = (cr // 2) % nz
    iy = cr // (2 * nz)
    rows = snaps // 2

    def x_peer(k):
        return ((sx + k) % nx, cr)

    def y_peer(k):
        return (sx, (((iy + k) % ny) * nz + iz) * 2 + core)

    def z_peer(k):
        return (sx, (iy * nz + (iz + k) % nz) * 2 + core)

    twin = (sx, cr + 1 - 2 * core)
    up = (sx, (cr + 1) % nc)
    down = (sx, (cr + nc - 1) % nc)

    def load(b):
        c, x = b % comps, (b // comps + xl - 2) % xl
        return pltpu.make_async_copy(vel.at[:, c, x], raw.at[b], load_sem.at[b])

    @pl.loop(0, comps * xl)
    def _(b):
        load(b).start()

    barrier = pltpu.get_barrier_semaphore()
    peers = [x_peer(k) for k in range(1, nx)] + [y_peer(k) for k in range(1, ny)]
    peers += [z_peer(k) for k in range(1, nz)] + [twin, up, down]
    for peer in peers:
        pl.semaphore_signal(barrier, inc=1, device_id=peer, device_id_type=MESH)

    @pl.when(sx == 0)
    def _():
        tiles[:, 0:2, 2 : yl + 2] = jnp.zeros((comps, 2, yl, snaps, cz), BF16)

    @pl.when(sx == nx - 1)
    def _():
        tiles[:, xl + 2 : xl + 4, 2 : yl + 2] = jnp.zeros((comps, 2, yl, snaps, cz), BF16)

    @pl.when(cr == 0)
    def _():
        tiles[:, 2 : xl + 2, 0:2] = jnp.zeros((comps, xl, 2, snaps, cz), BF16)

    @pl.when(cr == nc - 1)
    def _():
        tiles[:, 2 : xl + 2, yl + 2 : yl + 4] = jnp.zeros((comps, xl, 2, snaps, cz), BF16)

    pl.semaphore_wait(barrier, len(peers))

    def turn(b):
        c, x = b % comps, (b // comps + xl - 2) % xl
        load(b).wait()
        wide[...] = raw[b].astype(F32).reshape(snaps * yl, cz)
        for y in range(yl):
            tiles[c, x + 2, y + 2] = wide[pl.ds(y, snaps, stride=yl), :].astype(BF16)

    def remote(src, dst, send, recv, peer):
        return pltpu.make_async_remote_copy(
            src_ref=src, dst_ref=dst, send_sem=send, recv_sem=recv,
            device_id=peer, device_id_type=MESH,
        )

    right = ((sx + 1) % nx, cr)
    left = ((sx + nx - 1) % nx, cr)
    inner = pl.ds(2, yl)

    def x_right(c, r):
        return remote(
            tiles.at[c, xl + r, inner], tiles.at[c, r, inner],
            xs_sem.at[0, c, r], xr_sem.at[0, c, r], right,
        )

    def x_left(c, r):
        return remote(
            tiles.at[c, 2 + r, inner], tiles.at[c, xl + 2 + r, inner],
            xs_sem.at[1, c, r], xr_sem.at[1, c, r], left,
        )

    last = comps - 1

    def x_right_last(y):
        return remote(
            tiles.at[last, pl.ds(xl, 2), y + 2], tiles.at[last, pl.ds(0, 2), y + 2],
            xs2_sem.at[0, y], xr2_sem.at[0, y], right,
        )

    def x_left_last(y):
        return remote(
            tiles.at[last, pl.ds(2, 2), y + 2], tiles.at[last, pl.ds(xl + 2, 2), y + 2],
            xs2_sem.at[1, y], xr2_sem.at[1, y], left,
        )

    def y_up(c, x):
        return remote(
            tiles.at[c, x + 2, pl.ds(yl, 2)], tiles.at[c, x + 2, pl.ds(0, 2)],
            ys_sem.at[0, c, x], yr_sem.at[0, c, x], up,
        )

    def y_down(c, x):
        return remote(
            tiles.at[c, x + 2, pl.ds(2, 2)], tiles.at[c, x + 2, pl.ds(yl + 2, 2)],
            ys_sem.at[1, c, x], yr_sem.at[1, c, x], down,
        )

    has_right, has_left = sx < nx - 1, sx > 0
    has_up, has_down = cr < nc - 1, cr > 0

    @pl.loop(0, 2)
    def _(r):
        @pl.loop(0, comps)
        def _(c):
            turn(r * comps + c)

            @pl.when(jnp.logical_and(has_right, c < last))
            def _():
                x_right(c, r).start()

            turn((r + 2) * comps + c)

            @pl.when(jnp.logical_and(has_left, c < last))
            def _():
                x_left(c, r).start()

    @pl.loop(0, yl)
    def _(y):
        @pl.when(has_right)
        def _():
            x_right_last(y).start()

        @pl.when(has_left)
        def _():
            x_left_last(y).start()

    def send_y(c, x):
        @pl.when(has_up)
        def _():
            y_up(c, x).start()

        @pl.when(has_down)
        def _():
            y_down(c, x).start()

    @pl.loop(4 * comps, xl * comps)
    def _(b):
        turn(b)
        send_y(b % comps, b // comps - 2)

    @pl.loop(0, 4 * comps)
    def _(b):
        send_y(b % comps, (b // comps + xl - 2) % xl)

    acc[...] = jnp.zeros_like(acc)
    step = 32

    def unit(x, y):
        px, py = x + 2, y + 2
        scale_x = mx[x] * F32(1.0 / 12.0)
        scale_y = my[y] * F32(1.0 / 12.0)
        for c in range(comps):
            dz[c] = jnp.dot(tiles[c, px, py], sz[...], preferred_element_type=F32) * mz[...]
        for s in range(0, snaps, step):
            part_rows = slice(s, s + step)

            def at(c, i, j):
                return tiles[c, px + i, py + j, part_rows].astype(F32)

            def along_x(c):
                return (8.0 * (at(c, 1, 0) - at(c, -1, 0)) - (at(c, 2, 0) - at(c, -2, 0))) * scale_x

            def along_y(c):
                return (8.0 * (at(c, 0, 1) - at(c, 0, -1)) - (at(c, 0, 2) - at(c, 0, -2))) * scale_y

            stack[x, y, 0, part_rows] = (along_y(2) - dz[1, part_rows]).astype(BF16)
            stack[x, y, 1, part_rows] = (dz[0, part_rows] - along_x(2)).astype(BF16)
            stack[x, y, 2, part_rows] = (along_x(1) - along_y(0)).astype(BF16)
            stack[x, y, 3, part_rows] = (along_x(0) + along_y(1) + dz[2, part_rows]).astype(BF16)
        both = (((1,), (1,)), ((), ()))
        total = acc[...]
        for f in range(4):
            cells = stack[x, y, f]
            total += lax.dot_general(cells, cells, both, preferred_element_type=F32)
        acc[...] = total

    def put(x):
        return pltpu.make_async_copy(stack.at[x], x_out.at[x], out_sem.at[x])

    def wait_y(x):
        for c in range(comps):
            @pl.when(has_down)
            def _():
                y_up(c, x).wait_recv()

            @pl.when(has_up)
            def _():
                y_down(c, x).wait_recv()

    @pl.loop(2, xl - 2)
    def _(x):
        wait_y(x)

        @pl.loop(0, yl)
        def _(y):
            unit(x, y)

        put(x).start()

    @pl.loop(0, 4)
    def _(i):
        wait_y((i + xl - 2) % xl)

    for c in range(last):
        for r in range(2):
            @pl.when(has_left)
            def _():
                x_right(c, r).wait_recv()

            @pl.when(has_right)
            def _():
                x_left(c, r).wait_recv()

    @pl.loop(0, yl)
    def _(y):
        @pl.when(has_left)
        def _():
            x_right_last(y).wait_recv()

        @pl.when(has_right)
        def _():
            x_left_last(y).wait_recv()

        @pl.loop(0, 4)
        def _(i):
            unit((i + xl - 2) % xl, y)

    @pl.loop(0, 4)
    def _(i):
        put((i + xl - 2) % xl).start()

    mine = pl.ds(pl.multiple_of(core * rows, rows), rows)
    other = pl.ds(pl.multiple_of((1 - core) * rows, rows), rows)
    swap = remote(acc.at[other], half, cs_sem, cr_sem, twin)
    swap.start()
    swap.wait()
    value = acc[mine, :] + half[...]
    stages = ((sx, nx, x_peer), (iy, ny, y_peer), (iz, nz, z_peer))
    for a, (me, count, peer) in enumerate(stages):
        part[a, me] = value
        copies = [
            remote(part.at[a, me], part.at[a, me], as_sem.at[a, k - 1], ar_sem.at[a, k - 1], peer(k))
            for k in range(1, count)
        ]
        for copy in copies:
            copy.start()
        for k in range(1, count):
            source = (me + count - k) % count
            remote(
                part.at[a, me], part.at[a, source], as_sem.at[a, k - 1], ar_sem.at[a, k - 1], peer(k)
            ).wait_recv()
        value = part[a, 0]
        for k in range(1, count):
            value = value + part[a, k]
        for copy in copies:
            copy.wait_send()
    whole[mine, :] = value
    final = remote(whole.at[mine], whole.at[mine], fs_sem, fr_sem, twin)
    final.start()
    final.wait_send()
    remote(whole.at[mine], whole.at[other], fs_sem, fr_sem, twin).wait_recv()
    gram_out[...] = whole[...]

    @pl.loop(0, xl)
    def _(x):
        put(x).wait()

    @pl.loop(0, comps * xl)
    def _(b):
        c, x = b % comps, b // comps

        @pl.when(has_up)
        def _():
            y_up(c, x).wait_send()

        @pl.when(has_down)
        def _():
            y_down(c, x).wait_send()

    for c in range(last):
        for r in range(2):
            @pl.when(has_right)
            def _():
                x_right(c, r).wait_send()

            @pl.when(has_left)
            def _():
                x_left(c, r).wait_send()

    @pl.loop(0, yl)
    def _(y):
        @pl.when(has_right)
        def _():
            x_right_last(y).wait_send()

        @pl.when(has_left)
        def _():
            x_left_last(y).wait_send()


def factorise(gram, work, upper, inverse):
    count = gram.shape[0]
    work[...] = gram
    lane = lax.broadcasted_iota(jnp.int32, (PANEL, count), 1)
    sub = lax.broadcasted_iota(jnp.int32, (PANEL, count), 0)
    for k0 in range(0, count, PANEL):
        rows = slice(k0, k0 + PANEL)
        block = work[rows, :]
        cols = [jnp.broadcast_to(block[:, k0 + j : k0 + j + 1], (PANEL, count)) for j in range(PANEL)]
        pivots = jnp.zeros((PANEL, count), F32)
        for j in range(PANEL):
            pivot = jnp.broadcast_to(cols[j][j : j + 1, :], (PANEL, count))
            row = jnp.broadcast_to(block[j : j + 1, :], (PANEL, count))
            pivots = jnp.where(sub == j, pivot, pivots)
            times = jnp.where(sub > j, cols[j] / pivot, 0.0)
            for i in range(j + 1, PANEL):
                cols[i] = cols[i] - times * jnp.broadcast_to(cols[i][j : j + 1, :], (PANEL, count))
            block = jnp.where(
                jnp.logical_and(lane == k0 + j, sub > j), -times, block - times * row
            )
        root = lax.rsqrt(pivots)
        upper[rows, :] = jnp.where(lane >= k0 + sub, block * root, 0.0)
        in_panel = jnp.logical_and(lane >= k0, lane < k0 + PANEL)
        left = jnp.where(
            lane == k0 + sub, 1.0, jnp.where(jnp.logical_and(in_panel, lane > k0 + sub), 0.0, block)
        )
        inverse[rows, :] = jnp.where(lane <= k0 + sub, left * root, 0.0).astype(inverse.dtype)
        if k0 + PANEL < count:
            below = slice(k0 + PANEL, count)
            times = jnp.where(lane >= k0 + PANEL, block / pivots, 0.0)
            change = lax.dot_general(
                times, left, (((0,), (0,)), ((), ())),
                preferred_element_type=F32, precision=lax.Precision.HIGHEST,
            )
            wide_lane = lax.broadcasted_iota(jnp.int32, (count - k0 - PANEL, count), 1)
            kept = jnp.where(
                jnp.logical_and(wide_lane >= k0, wide_lane < k0 + PANEL), 0.0, work[below, :]
            )
            work[below, :] = kept - change[k0 + PANEL :, :]


def modes_kernel(scale, gram, x, modes, factor, work, upper, inverse, wide):
    snaps, fields, _, yl, cz = modes.shape

    @pl.when(pl.program_id(0) == 0)
    def _():
        factorise(gram[...] * F32(scale), work, upper, inverse)
        factor[...] = upper[...].T

    for f in range(fields):
        for y in range(yl):
            wide[pl.ds(y, snaps, stride=yl), :] = jnp.dot(
                inverse[...], x[0, y, f], preferred_element_type=F32
            )
        modes[:, f, 0] = wide[...].reshape(snaps, yl, cz).astype(BF16)


def shards(sizes, velocity, metric_x, metric_y, metric_z):
    snaps, comps, xl, yl, cz = velocity.shape
    nx, ny, nz = sizes
    lanes = jnp.arange(cz)
    apart = lanes[:, None] - lanes[None, :]
    sz = (
        8.0 * (apart == 1) - 8.0 * (apart == -1) - 1.0 * (apart == 2) + 1.0 * (apart == -2)
    ).astype(BF16)
    mz = (metric_z * (1.0 / 12.0)).reshape(1, cz)
    rows = snaps // 2
    dma = pltpu.SemaphoreType.DMA
    most = max(sizes)
    stack, gram = pl.pallas_call(
        functools.partial(gram_kernel, sizes),
        out_shape=(
            jax.ShapeDtypeStruct((xl, yl, 4, snaps, cz), BF16),
            jax.ShapeDtypeStruct((snaps, snaps), F32),
        ),
        in_specs=[
            pl.BlockSpec(memory_space=pl.ANY),
            pl.BlockSpec(memory_space=pltpu.SMEM),
            pl.BlockSpec(memory_space=pltpu.SMEM),
            pl.BlockSpec(memory_space=pltpu.VMEM),
            pl.BlockSpec(memory_space=pltpu.VMEM),
        ],
        out_specs=(pl.BlockSpec(memory_space=pl.ANY), pl.BlockSpec(memory_space=pltpu.VMEM)),
        scratch_shapes=[
            pltpu.VMEM((comps * xl, snaps, yl, cz), BF16),
            pltpu.VMEM((comps, xl + 4, yl + 4, snaps, cz), BF16),
            pltpu.VMEM((xl, yl, 4, snaps, cz), BF16),
            pltpu.VMEM((snaps * yl, cz), F32),
            pltpu.VMEM((comps, snaps, cz), F32),
            pltpu.VMEM((snaps, snaps), F32),
            pltpu.VMEM((rows, snaps), F32),
            pltpu.VMEM((3, most, rows, snaps), F32),
            pltpu.VMEM((snaps, snaps), F32),
            dma((comps * xl,)),
            dma((xl,)),
            dma((2, comps - 1, 2)),
            dma((2, comps - 1, 2)),
            dma((2, yl)),
            dma((2, yl)),
            dma((2, comps, xl)),
            dma((2, comps, xl)),
            dma,
            dma,
            dma((3, most)),
            dma((3, most)),
            dma,
            dma,
        ],
        compiler_params=pltpu.CompilerParams(
            collective_id=0, has_side_effects=True, vmem_limit_bytes=VMEM_LIMIT
        ),
        name="fields_gram",
    )(velocity, metric_x, metric_y, mz, sz)
    scale = 1.0 / (4.0 * xl * nx * yl * ny * nz * 2 * cz)
    return pl.pallas_call(
        functools.partial(modes_kernel, scale),
        grid=(xl,),
        out_shape=(
            jax.ShapeDtypeStruct((snaps, 4, xl, yl, cz), BF16),
            jax.ShapeDtypeStruct((snaps, snaps), F32),
        ),
        in_specs=[
            pl.BlockSpec((snaps, snaps), lambda i: (0, 0)),
            pl.BlockSpec((1, yl, 4, snaps, cz), lambda i: (i, 0, 0, 0, 0)),
        ],
        out_specs=(
            pl.BlockSpec((snaps, 4, 1, yl, cz), lambda i: (0, 0, i, 0, 0)),
            pl.BlockSpec((snaps, snaps), lambda i: (0, 0)),
        ),
        scratch_shapes=[
            pltpu.VMEM((snaps, snaps), F32),
            pltpu.VMEM((snaps, snaps), F32),
            pltpu.VMEM((snaps, snaps), BF16),
            pltpu.VMEM((snaps * yl, cz), F32),
        ],
        compiler_params=pltpu.CompilerParams(
            dimension_semantics=("arbitrary",), vmem_limit_bytes=VMEM_LIMIT
        ),
        name="factor_modes",
    )(gram, stack)


def solution(mesh):
    across = mesh.shape["cross"]
    nz = 4 if across >= 32 else 2
    sizes = (mesh.shape["stream"], across // (2 * nz), nz)
    return jax.shard_map(
        functools.partial(shards, sizes),
        mesh=mesh,
        in_specs=(P(None, None, "stream", "cross", None), P("stream"), P("cross"), P()),
        out_specs=(P(None, None, "stream", "cross", None), P()),
        check_vma=False,
    )
```

time: 444 us -> 97.6 us (0.22)
  waiting for transfers between devices: 214 us -> 0 us
  other arithmetic: 104 us -> 1.82 us
  Pallas kernels: 0 us -> 94.6 us
  local copies, waits for them, and re-layouts: 71.8 us -> 0 us
  matrix products: 24.9 us -> 0 us
  between operations: 14.1 us -> 0.64 us
  starting transfers between devices: 12.5 us -> 0 us
    psum x1 -> x0, waiting for transfers between devices: 141 us -> none  [global_factor(): gram = lax.psum(local, ('stream', 'cross'))]
    pallas_call x0 -> x2, Pallas kernels: none -> 94.6 us  [the longest x1 71.4 us: shards(): pl.pallas_call(functools.partial(gram_kernel, sizes), out_shape=(jax.Shap...]
    ppermute x4 -> x0, waiting for transfers between devices: 72.5 us -> none  [the longest x2 64.2 us: with_halo(): lax.ppermute(tail, axis, [(i, (i + 1) % count) for i in range(ends)])]
    another operation x53 -> x0, other arithmetic: 45.2 us -> none  [the longest x48 21.7 us: fields(): jnp.stack([vort_x, vort_y, vort_z, dilatation], axis=1).astype(jnp.bfloat16)]
    dynamic_slice x32 -> x0, local copies, waits for them, and re-layouts: 30 us -> none  [shards(): stacked = lax.map(one_block, padded_groups)]
    dot_general x2 -> x0, matrix products: 24.7 us -> none  [the longest x1 12.5 us: shards(): jnp.dot(inverse.astype(jnp.bfloat16), flat, preferred_element_type=jnp.fl...]
    concatenate x1 -> x0, other arithmetic: 19.7 us -> none  [with_halo(): jnp.concatenate([lax.ppermute(tail, axis, [(i, (i + 1) % count) for i in...]
    unnamed x10 -> x0, local copies, waits for them, and re-layouts: 18.6 us -> none
  transfers between devices with their start and end apart: 5 -> 0, of which waited for: 5 -> 0; matrix products, arithmetic and copies ran while one was open for 0% -> 0% of each run, Pallas kernels for 0% -> 0%
where the time goes in v1:
time: 97.6 us; the launch traced here: 97 us
  Pallas kernels  94.6 us (97%)
  other arithmetic  1.82 us (2%)
    pallas_call x1, Pallas kernels, shards(): pl.pallas_call(functools.partial(gram_kernel, sizes), out_shape=(jax.Shap...  71.4 us
    pallas_call x1, Pallas kernels, shards(): pl.pallas_call(functools.partial(modes_kernel, scale), grid=(xl,), out_sh...  23.1 us

profile of v1, /device:TPU:1, one launch (start us, length us, event | category | flops | bytes accessed | tf_op | source)
XLA Modules:
  0.0 97.0 jit_solution(2405591657345829073)
XLA Ops:
  0.6 1.2 %multiply_bitcast_fusion.mz = f32[1,128]{1,0:T(1,128)} fusion(f32[128]{0:T(128)} %param.7), kind=kLoop, calls=%fused_computation.6 | loop fusion | flops 128 | bytes 1024 | tf_op jit(solution)/shard_map/reshape | solution.py:402
  1.8 0.6 add_convert_fusion.sz
  2.4 71.4 %fields_gram.1 = (bf16[12,8,4,128,128]{4,3,2,1,0:T(8,128)(2,1)}, f32[128,128]{1,0:T(8,128)}) custom-call(bf16[128,3,12,8,128]{4,3,2,1,0:T(8,128)(2,1)} %vel.1, f32[12]{0:T(128)} %mx.1, f32[8]{0:T(128)} %my.1, f32[1,128]{1,0:T(1,128)} %multiply_bitcast_fusion.mz, bf16[128,128]{1,0:T(8,128)(2,1)} %add_convert_fusion.sz), custom_call_target="tpu_custom_call" | custom-call | tf_op jit(solution)/shard_map/fields_gram/pallas_call | solution.py:406
  73.9 23.1 %factor_modes.1 = (bf16[128,4,12,8,128]{4,3,2,1,0:T(8,128)(2,1)}, f32[128,128]{1,0:T(8,128)}) custom-call(f32[128,128]{1,0:T(8,128)} %get-tuple-element.4.gram, bf16[12,8,4,128,128]{4,3,2,1,0:T(8,128)(2,1)} %get-tuple-element.5.x), custom_call_target="tpu_custom_call" | custom-call | tf_op jit(solution)/shard_map/factor_modes/pallas_call | solution.py:451

commit v2 on v1

--- a/solution.py
+++ b/solution.py
@@ -181,34 +181,51 @@
     acc[...] = jnp.zeros_like(acc)
     step = 32
 
-    def unit(x, y):
+    def fields(slot, x, y):
         px, py = x + 2, y + 2
         scale_x = mx[x] * F32(1.0 / 12.0)
-        scale_y = my[y] * F32(1.0 / 12.0)
-        for c in range(comps):
-            dz[c] = jnp.dot(tiles[c, px, py], sz[...], preferred_element_type=F32) * mz[...]
         for s in range(0, snaps, step):
             part_rows = slice(s, s + step)
+            scale_y = [my[y + k] * F32(1.0 / 12.0) for k in range(2)]
 
             def at(c, i, j):
                 return tiles[c, px + i, py + j, part_rows].astype(F32)
 
-            def along_x(c):
-                return (8.0 * (at(c, 1, 0) - at(c, -1, 0)) - (at(c, 2, 0) - at(c, -2, 0))) * scale_x
-
-            def along_y(c):
-                return (8.0 * (at(c, 0, 1) - at(c, 0, -1)) - (at(c, 0, 2) - at(c, 0, -2))) * scale_y
-
-            stack[x, y, 0, part_rows] = (along_y(2) - dz[1, part_rows]).astype(BF16)
-            stack[x, y, 1, part_rows] = (dz[0, part_rows] - along_x(2)).astype(BF16)
-            stack[x, y, 2, part_rows] = (along_x(1) - along_y(0)).astype(BF16)
-            stack[x, y, 3, part_rows] = (along_x(0) + along_y(1) + dz[2, part_rows]).astype(BF16)
+            column = [[at(c, 0, j) for j in range(-2, 4)] for c in range(comps)]
+
+            def along_x(c, k):
+                return (8.0 * (at(c, 1, k) - at(c, -1, k)) - (at(c, 2, k) - at(c, -2, k))) * scale_x
+
+            def along_y(c, k):
+                f = column[c][k : k + 5]
+                return (8.0 * (f[3] - f[1]) - (f[4] - f[0])) * scale_y[k]
+
+            for k in range(2):
+                along_z = [dz[slot, c, part_rows, k * cz : (k + 1) * cz] for c in range(comps)]
+                stack[x, y + k, 0, part_rows] = (along_y(2, k) - along_z[1]).astype(BF16)
+                stack[x, y + k, 1, part_rows] = (along_z[0] - along_x(2, k)).astype(BF16)
+                stack[x, y + k, 2, part_rows] = (along_x(1, k) - along_y(0, k)).astype(BF16)
+                stack[x, y + k, 3, part_rows] = (
+                    along_x(0, k) + along_y(1, k) + along_z[2]
+                ).astype(BF16)
+
+    def products(x, y):
         both = (((1,), (1,)), ((), ()))
         total = acc[...]
-        for f in range(4):
-            cells = stack[x, y, f]
-            total += lax.dot_general(cells, cells, both, preferred_element_type=F32)
+        for k in range(2):
+            for f in range(0, 4, 2):
+                cells = jnp.concatenate([stack[x, y + k, f], stack[x, y + k, f + 1]], axis=1)
+                total += lax.dot_general(cells, cells, both, preferred_element_type=F32)
         acc[...] = total
+
+    def units(*cells):
+        for slot, (x, y) in enumerate(cells):
+            for c in range(comps):
+                pair = jnp.concatenate([tiles[c, x + 2, y + 2], tiles[c, x + 2, y + 3]], axis=1)
+                dz[slot, c] = jnp.dot(pair, sz[...], preferred_element_type=F32) * mz[...]
+        for slot, (x, y) in enumerate(cells):
+            fields(slot, x, y)
+            products(x, y)
 
     def put(x):
         return pltpu.make_async_copy(stack.at[x], x_out.at[x], out_sem.at[x])
@@ -227,9 +244,9 @@
     def _(x):
         wait_y(x)
 
-        @pl.loop(0, yl)
-        def _(y):
-            unit(x, y)
+        @pl.loop(0, yl // 4)
+        def _(h):
+            units((x, 4 * h), (x, 4 * h + 2))
 
         put(x).start()
 
@@ -247,19 +264,20 @@
             def _():
                 x_left(c, r).wait_recv()
 
-    @pl.loop(0, yl)
-    def _(y):
-        @pl.when(has_left)
-        def _():
-            x_right_last(y).wait_recv()
-
-        @pl.when(has_right)
-        def _():
-            x_left_last(y).wait_recv()
-
-        @pl.loop(0, 4)
+    @pl.loop(0, yl // 2)
+    def _(h):
+        for k in range(2):
+            @pl.when(has_left)
+            def _():
+                x_right_last(2 * h + k).wait_recv()
+
+            @pl.when(has_right)
+            def _():
+                x_left_last(2 * h + k).wait_recv()
+
+        @pl.loop(0, 2)
         def _(i):
-            unit((i + xl - 2) % xl, y)
+            units(((2 * i + xl - 2) % xl, 2 * h), ((2 * i + xl - 1) % xl, 2 * h))
 
     @pl.loop(0, 4)
     def _(i):
@@ -394,12 +412,14 @@
 def shards(sizes, velocity, metric_x, metric_y, metric_z):
     snaps, comps, xl, yl, cz = velocity.shape
     nx, ny, nz = sizes
-    lanes = jnp.arange(cz)
+    lanes = jnp.arange(2 * cz)
     apart = lanes[:, None] - lanes[None, :]
-    sz = (
+    same = lanes[:, None] // cz == lanes[None, :] // cz
+    sz = same * (
         8.0 * (apart == 1) - 8.0 * (apart == -1) - 1.0 * (apart == 2) + 1.0 * (apart == -2)
-    ).astype(BF16)
-    mz = (metric_z * (1.0 / 12.0)).reshape(1, cz)
+    )
+    sz = sz.astype(BF16)
+    mz = jnp.tile((metric_z * (1.0 / 12.0)).reshape(1, cz), (1, 2))
     rows = snaps // 2
     dma = pltpu.SemaphoreType.DMA
     most = max(sizes)
@@ -422,7 +442,7 @@
             pltpu.VMEM((comps, xl + 4, yl + 4, snaps, cz), BF16),
             pltpu.VMEM((xl, yl, 4, snaps, cz), BF16),
             pltpu.VMEM((snaps * yl, cz), F32),
-            pltpu.VMEM((comps, snaps, cz), F32),
+            pltpu.VMEM((2, comps, snaps, 2 * cz), F32),
             pltpu.VMEM((snaps, snaps), F32),
             pltpu.VMEM((rows, snaps), F32),
             pltpu.VMEM((3, most, rows, snaps), F32),

time: 97.6 us -> 91.6 us (0.939)
  Pallas kernels: 94.6 us -> 88.5 us
    pallas_call x1, Pallas kernels: 71.4 us -> 65.4 us  [shards(): pl.pallas_call(functools.partial(gram_kernel, sizes), out_shape=(jax.Shap...]
    reshape x1 -> x0, other arithmetic: 1.17 us -> none  [shards(): mz = (metric_z * (1.0 / 12.0)).reshape(1, cz)]
where the time goes in v2:
time: 91.6 us; the launch traced here: 91.1 us
  Pallas kernels  88.5 us (97%)
  other arithmetic  1.42 us (2%)
    pallas_call x1, Pallas kernels, shards(): pl.pallas_call(functools.partial(gram_kernel, sizes), out_shape=(jax.Shap...  65.4 us
    pallas_call x1, Pallas kernels, shards(): pl.pallas_call(functools.partial(modes_kernel, scale), grid=(xl,), out_sh...  23.1 us

profile of v2, /device:TPU:1, one launch (start us, length us, event | category | flops | bytes accessed | tf_op | source)
XLA Modules:
  0.0 91.1 jit_solution(2600953223337543716)
XLA Ops:
  0.6 0.7 broadcast_multiply_fusion
  1.3 0.6 tile.8
  1.9 0.8 select_convert_fusion.sz
  2.6 65.4 %fields_gram.1 = (bf16[12,8,4,128,128]{4,3,2,1,0:T(8,128)(2,1)}, f32[128,128]{1,0:T(8,128)}) custom-call(bf16[128,3,12,8,128]{4,3,2,1,0:T(8,128)(2,1)} %vel.1, f32[12]{0:T(128)} %mx.1, f32[8]{0:T(128)} %my.1, f32[1,256]{1,0:T(1,128)} %bitcast.1, bf16[256,256]{1,0:T(8,128)(2,1)} %select_convert_fusion.sz), custom_call_target="tpu_custom_call" | custom-call | tf_op jit(solution)/shard_map/fields_gram/pallas_call | solution.py:426
  68.0 23.1 %factor_modes.1 = (bf16[128,4,12,8,128]{4,3,2,1,0:T(8,128)(2,1)}, f32[128,128]{1,0:T(8,128)}) custom-call(f32[128,128]{1,0:T(8,128)} %get-tuple-element.4.gram, bf16[12,8,4,128,128]{4,3,2,1,0:T(8,128)(2,1)} %get-tuple-element.5.x), custom_call_target="tpu_custom_call" | custom-call | tf_op jit(solution)/shard_map/factor_modes/pallas_call | solution.py:471
  (1 shorter events, 0.0 us)

commit v3 on v2

--- a/solution.py
+++ b/solution.py
@@ -2,6 +2,7 @@
 
 import jax
 import jax.numpy as jnp
+import numpy as np
 from jax import lax
 from jax.experimental import pallas as pl
 from jax.experimental.pallas import tpu as pltpu
@@ -16,7 +17,7 @@
 
 def gram_kernel(
     sizes, vel, mx, my, mz, sz, x_out, gram_out,
-    raw, tiles, stack, wide, dz, acc, half, part, whole,
+    raw, tiles, stack, wide, scale_z, dz, acc, half, part, whole,
     load_sem, out_sem, xs_sem, xr_sem, xs2_sem, xr2_sem, ys_sem, yr_sem,
     cs_sem, cr_sem, as_sem, ar_sem, fs_sem, fr_sem,
 ):
@@ -179,6 +180,8 @@
         send_y(b % comps, (b // comps + xl - 2) % xl)
 
     acc[...] = jnp.zeros_like(acc)
+    scale_z[:, :cz] = mz[...] * F32(1.0 / 12.0)
+    scale_z[:, cz:] = mz[...] * F32(1.0 / 12.0)
     step = 32
 
     def fields(slot, x, y):
@@ -222,7 +225,7 @@
         for slot, (x, y) in enumerate(cells):
             for c in range(comps):
                 pair = jnp.concatenate([tiles[c, x + 2, y + 2], tiles[c, x + 2, y + 3]], axis=1)
-                dz[slot, c] = jnp.dot(pair, sz[...], preferred_element_type=F32) * mz[...]
+                dz[slot, c] = jnp.dot(pair, sz[...], preferred_element_type=F32) * scale_z[...]
         for slot, (x, y) in enumerate(cells):
             fields(slot, x, y)
             products(x, y)
@@ -393,33 +396,40 @@
             work[below, :] = kept - change[k0 + PANEL :, :]
 
 
-def modes_kernel(scale, gram, x, modes, factor, work, upper, inverse, wide):
-    snaps, fields, _, yl, cz = modes.shape
-
-    @pl.when(pl.program_id(0) == 0)
+def modes_kernel(scale, gram, x, modes, factor, work, upper, inverse, held, sem):
+    fields, yl = modes.shape[1], modes.shape[3]
+    cz = modes.shape[4]
+    step = pl.program_id(0)
+
+    def fetch(i):
+        return pltpu.make_async_copy(x.at[i], held.at[i], sem.at[i])
+
+    @pl.when(step == 0)
     def _():
+        for i in range(x.shape[0]):
+            fetch(i).start()
         factorise(gram[...] * F32(scale), work, upper, inverse)
         factor[...] = upper[...].T
 
+    fetch(step).wait()
     for f in range(fields):
-        for y in range(yl):
-            wide[pl.ds(y, snaps, stride=yl), :] = jnp.dot(
-                inverse[...], x[0, y, f], preferred_element_type=F32
-            )
-        modes[:, f, 0] = wide[...].reshape(snaps, yl, cz).astype(BF16)
+        rows = []
+        for y in range(0, yl, 2):
+            pair = jnp.concatenate([held[step, y, f], held[step, y + 1, f]], axis=1)
+            both = jnp.dot(inverse[...], pair, preferred_element_type=F32).astype(BF16)
+            rows += [both[:, :cz], both[:, cz:]]
+        modes[:, f, 0] = jnp.swapaxes(jnp.stack(rows, axis=0), 0, 1)
 
 
 def shards(sizes, velocity, metric_x, metric_y, metric_z):
     snaps, comps, xl, yl, cz = velocity.shape
     nx, ny, nz = sizes
-    lanes = jnp.arange(2 * cz)
+    lanes = np.arange(2 * cz)
     apart = lanes[:, None] - lanes[None, :]
     same = lanes[:, None] // cz == lanes[None, :] // cz
-    sz = same * (
-        8.0 * (apart == 1) - 8.0 * (apart == -1) - 1.0 * (apart == 2) + 1.0 * (apart == -2)
-    )
-    sz = sz.astype(BF16)
-    mz = jnp.tile((metric_z * (1.0 / 12.0)).reshape(1, cz), (1, 2))
+    stencil = 8.0 * (apart == 1) - 8.0 * (apart == -1) - 1.0 * (apart == 2) + 1.0 * (apart == -2)
+    sz = jnp.asarray(same * stencil, BF16)
+    mz = metric_z.reshape(1, cz)
     rows = snaps // 2
     dma = pltpu.SemaphoreType.DMA
     most = max(sizes)
@@ -442,6 +452,7 @@
             pltpu.VMEM((comps, xl + 4, yl + 4, snaps, cz), BF16),
             pltpu.VMEM((xl, yl, 4, snaps, cz), BF16),
             pltpu.VMEM((snaps * yl, cz), F32),
+            pltpu.VMEM((1, 2 * cz), F32),
             pltpu.VMEM((2, comps, snaps, 2 * cz), F32),
             pltpu.VMEM((snaps, snaps), F32),
             pltpu.VMEM((rows, snaps), F32),
@@ -477,7 +488,7 @@
         ),
         in_specs=[
             pl.BlockSpec((snaps, snaps), lambda i: (0, 0)),
-            pl.BlockSpec((1, yl, 4, snaps, cz), lambda i: (i, 0, 0, 0, 0)),
+            pl.BlockSpec(memory_space=pl.ANY),
         ],
         out_specs=(
             pl.BlockSpec((snaps, 4, 1, yl, cz), lambda i: (0, 0, i, 0, 0)),
@@ -487,7 +498,8 @@
             pltpu.VMEM((snaps, snaps), F32),
             pltpu.VMEM((snaps, snaps), F32),
             pltpu.VMEM((snaps, snaps), BF16),
-            pltpu.VMEM((snaps * yl, cz), F32),
+            pltpu.VMEM((xl, yl, 4, snaps, cz), BF16),
+            dma((xl,)),
         ],
         compiler_params=pltpu.CompilerParams(
             dimension_semantics=("arbitrary",), vmem_limit_bytes=VMEM_LIMIT

time: 91.6 us -> 84.9 us (0.927)
  Pallas kernels: 88.5 us -> 84 us
  other arithmetic: 1.42 us -> 0 us
    pallas_call x1, Pallas kernels: 23.1 us -> 18.6 us  [shards(): pl.pallas_call(functools.partial(modes_kernel, scale), grid=(xl,), out_sh...]
where the time goes in v3:
time: 84.9 us; the launch traced here: 84.7 us
  Pallas kernels  84 us (99%)
    pallas_call x1, Pallas kernels, shards(): pl.pallas_call(functools.partial(gram_kernel, sizes), out_shape=(jax.Shap...  65.4 us
    pallas_call x1, Pallas kernels, shards(): pl.pallas_call(functools.partial(modes_kernel, scale), grid=(xl,), out_sh...  18.6 us

profile of v3, /device:TPU:1, one launch (start us, length us, event | category | flops | bytes accessed | tf_op | source)
XLA Modules:
  0.0 84.7 jit_solution(12697058432666651627)
XLA Ops:
  0.6 65.4 %fields_gram.1 = (bf16[12,8,4,128,128]{4,3,2,1,0:T(8,128)(2,1)}, f32[128,128]{1,0:T(8,128)}) custom-call(bf16[128,3,12,8,128]{4,3,2,1,0:T(8,128)(2,1)} %vel.1, f32[12]{0:T(128)} %mx.1, f32[8]{0:T(128)} %my.1, f32[1,128]{1,0:T(1,128)} %bitcast.1, bf16[256,256]{1,0:T(8,128)(2,1)} %constant.2.clone.sz), custom_call_target="tpu_custom_call" | custom-call | tf_op jit(solution)/shard_map/fields_gram/pallas_call | solution.py:436
  66.1 18.6 %factor_modes.1 = (bf16[128,4,12,8,128]{4,3,2,1,0:T(8,128)(2,1)}, f32[128,128]{1,0:T(8,128)}) custom-call(f32[128,128]{1,0:T(8,128)} %get-tuple-element.4.gram, bf16[12,8,4,128,128]{4,3,2,1,0:T(8,128)(2,1)} %get-tuple-element.5.x), custom_call_target="tpu_custom_call" | custom-call | tf_op jit(solution)/shard_map/factor_modes/pallas_call | solution.py:482
